TPU v7x, 256 devices: a whole 4x4x8 slice. The times are simulated.
256 devices in a mesh: section: 32 (over z, y_hi, core), tp: 8 (over x, y_lo).
Axes of the slice: x: 4, y: 4 (y_hi: 2, y_lo: 2; y = y_hi * 2 + y_lo), z: 8, core: 2. Of those that a mesh axis runs over, the one named last changes fastest.
Arguments:
- block_input: bfloat16 [32, 2, 128, 4096], P('section', None, None, 'tp'), may hold values from -6 to 6
- incoming: bfloat16 [32, 2, 128, 4096], P('section', None, None, 'tp'), may hold values from -6 to 6
- in_weight: bfloat16 [32, 4096, 3, 4096], P('section', None, None, 'tp'), may hold values from -0.09375 to 0.09375
- short_taps: float32 [32, 7, 3, 4096], P('section', None, None, 'tp'), may hold values from -2.5 to 2.5
- medium_taps: float32 [32, 128, 256], P('section', None, 'tp'), may hold values from -0.625 to 0.625
- skip_weight: float32 [32, 4096], P('section', 'tp'), may hold values from 0.5 to 1.5
Outputs:
- passed: bfloat16 [32, 2, 128, 4096], P('section', None, None, 'tp')
All inputs are finite; a program needn't handle non-finite values.
Results may differ from a plain program's by a relative error of at most 0.0049.
Values may be sent and summed in bfloat16 or wider, within the bound.
A program may use at most 128 MiB of HBM per device.

v0:
```python
import jax
import jax.numpy as jnp
from jax import lax
from jax.sharding import PartitionSpec as P


def shifted(value, axis, steps):
    count = lax.axis_size(axis)
    pairs = [(source, (source + steps) % count) for source in range(count)]
    return lax.ppermute(value, axis, pairs)


def causal_taps(series, taps):
    length = series.shape[1]
    reach = taps.shape[0]
    padded = jnp.pad(series, ((0, 0), (reach - 1, 0), (0, 0), (0, 0)))
    result = jnp.zeros(series.shape, jnp.float32)
    for offset in range(reach):
        first = reach - 1 - offset
        result = result + taps[offset] * padded[:, first : first + length]
    return result


def anti_taps(series, taps):
    length = series.shape[1]
    reach = taps.shape[0]
    padded = jnp.pad(series, ((0, 0), (0, reach - 1), (0, 0), (0, 0)))
    result = jnp.zeros(series.shape, jnp.float32)
    for offset in range(reach):
        result = result + taps[offset] * padded[:, offset : offset + length]
    return result


def toeplitz_of(medium, length):
    reach = medium.shape[0]
    places = jnp.arange(length, dtype=jnp.int32)
    lag_table = places[:, None] - places[None, :]
    inside = (lag_table >= 0) & (lag_table < reach)
    lag_index = jnp.clip(lag_table, 0, reach - 1)
    looked = jnp.take(medium.T, lag_index, axis=1)
    return jnp.where(inside[None, :, :], looked, jnp.zeros((), jnp.float32))


def time_last(series, groups):
    micro_count, length, channels = series.shape
    turned = jnp.transpose(series, (0, 2, 1))
    return turned.reshape(micro_count, groups, channels // groups, length)


def time_back(series):
    micro_count, groups, members, length = series.shape
    merged = series.reshape(micro_count, groups * members, length)
    return jnp.transpose(merged, (0, 2, 1))


def section_backward(block_input, incoming, weights, short_taps, toeplitz_mat, skip_weight):
    micro_count = block_input.shape[1]
    length = block_input.shape[2]
    channels = skip_weight.shape[0]
    groups = toeplitz_mat.shape[0]
    portion = lax.all_gather(block_input, "tp", axis=3, tiled=True)
    slab_rows = weights
    flattened = portion.reshape(micro_count * length, portion.shape[3])
    projected = jnp.dot(flattened, slab_rows, preferred_element_type=jnp.float32)
    projected = projected.reshape(micro_count, length, 3, channels)
    featured = causal_taps(projected, short_taps)
    query = featured[:, :, 0]
    key_part = featured[:, :, 1]
    value_part = featured[:, :, 2]
    product = key_part * value_part
    grouped = time_last(product, groups)
    mixed = jnp.einsum("gts,bgcs->bgct", toeplitz_mat, grouped, precision=lax.Precision.HIGHEST)
    mixed = time_back(mixed) + skip_weight * product
    upstream = incoming[0].astype(jnp.float32)
    query_grad = upstream * mixed
    mixed_grad = upstream * query
    grouped_grad = time_last(mixed_grad, groups)
    product_grad = jnp.einsum(
        "gts,bgct->bgcs", toeplitz_mat, grouped_grad, precision=lax.Precision.HIGHEST
    )
    product_grad = time_back(product_grad) + skip_weight * mixed_grad
    stream_grad = jnp.stack(
        [query_grad, product_grad * value_part, product_grad * key_part], axis=2
    )
    conv_grad = anti_taps(stream_grad, short_taps).astype(jnp.bfloat16)
    conv_flat = conv_grad.reshape(micro_count * length, 3 * channels)
    slab_rows = weights
    own_share = lax.psum_scatter(
        lax.dot_general(
            slab_rows, conv_flat, (((1,), (1,)), ((), ())), preferred_element_type=jnp.float32
        ),
        "tp",
        scatter_dimension=0,
        tiled=True,
    )
    summed = upstream + own_share.T.reshape(micro_count, length, channels)
    result = summed.astype(jnp.bfloat16)[None]
    return shifted(result, "section", -1)


def local(block_input, incoming, in_weight, short_taps, medium_taps, skip_weight):
    model_width = in_weight.shape[1]
    channels = in_weight.shape[3]
    weights = in_weight[0].reshape(model_width, 3 * channels)
    toeplitz_mat = toeplitz_of(medium_taps[0], block_input.shape[2])
    return section_backward(
        block_input, incoming, weights, short_taps[0], toeplitz_mat, skip_weight[0]
    )


def solution(mesh):
    in_specs = (
        P("section", None, None, "tp"),
        P("section", None, None, "tp"),
        P("section", None, None, "tp"),
        P("section", None, None, "tp"),
        P("section", None, "tp"),
        P("section", "tp"),
    )
    out_specs = P("section", None, None, "tp")
    return jax.shard_map(local, mesh=mesh, in_specs=in_specs, out_specs=out_specs, check_vma=False)
```

profile of v0, /device:TPU:1, one launch (start us, length us, event | category | flops | bytes accessed | tf_op | source)
XLA Modules:
  0.0 230.5 jit_solution(18005808708087113482)
XLA Ops:
  6.5 0.7 all-gather.2.cloned.1.call-update
  7.3 0.0 reduce-scatter.2.cloned.1.call-start
  7.3 17.0 %copy.23 = bf16[1,4096,3,512]{1,3,2,0:T(8,128)(2,1)} copy(bf16[1,4096,3,512]{3,1,2,0:T(8,128)(2,1)} %param.8) | data formatting | bytes 25165824 | tf_op args[2]
  24.3 0.1 copy.35
  24.5 54.4 %gather_fusion = f32[16384,32]{1,0:T(8,128)} fusion(f32[32,128]{0,1:T(8,128)S(1)} %bitcast.146, s32[16384]{0:T(1024)S(1)} %fusion.40), kind=kCustom, calls=%fused_computation | custom fusion | bytes 4259840 | tf_op jit(solution)/shard_map/jit(_take)/gather | solution.py:40
  78.8 5.5 %copy.36 = f32[128,128,32]{1,0,2:T(8,128)S(1)} copy(f32[128,128,32]{2,1,0:T(8,128)} %bitcast.148) | data formatting | bytes 4194304 | tf_op jit(solution)/shard_map/jit(_take)/gather | solution.py:40
  84.5 0.0 all-gather.2.cloned.1.call-done
  84.5 7.2 %fusion = f32[2,128,3,512]{3,1,2,0:T(8,128)S(1)} fusion(bf16[1,4096,3,512]{1,3,2,0:T(8,128)(2,1)} %copy.23, bf16[1,2,128,4096]{3,2,1,0:T(8,128)(2,1)} %all-gather.2.cloned.1.call-done), kind=kOutput, calls=%fused_computation.1 | convolution fusion | flops 3221225472 | bytes 16252928 | tf_op jit(solution)/shard_map/dot_general | solution.py:64
  91.6 1.0 pad_slice_fusion.4
  92.7 1.3 copy_add_fusion
  93.9 1.2 copy-done
  95.1 1.0 fusion.38
  96.1 1.2 copy.40
  97.4 2.0 fusion.17
  99.4 1.0 copy.43
  100.4 0.2 copy.34
  100.6 3.4 %fusion.14 = f32[2,32,16,128]{3,2,0,1:T(8,128)S(1)} fusion(f32[128,128,32]{1,0,2:T(8,128)S(1)} %copy.36, pred[128,128]{1,0:T(8,128)(4,1)S(1)} %get-tuple-element.29, pred[128,128]{1,0:T(8,128)(4,1)S(1)} %get-tuple-element.28, f32[2,32,16,128]{3,2,1,0:T(8,128)S(1)} %bitcast.150), kind=kOutput, calls=%fused_computation.32 | convolution fusion | flops 202375168 | bytes 3178496 | tf_op jit(solution)/shard_map/gts,bgcs->bgct/dot_general | solution.py:72
  104.0 0.0 copy-start.6
  104.0 0.2 copy.39
  104.2 1.1 copy-done.1
  105.4 0.1 copy-done.3
  105.5 0.3 multiply_bitcast_fusion.1
  105.8 0.1 pad_maximum_fusion
  105.9 1.3 add_convert_fusion
  107.2 0.6 copy.44
  107.9 9.7 %convolution_bitcast_fusion = f32[4096,256]{0,1:T(8,128)} fusion(bf16[4096,1536]{0,1:T(8,128)(2,1)} %bitcast.147, bf16[192,8,2,128]{3,2,1,0:T(2,128)(2,1)S(1)} %bitcast.149), kind=kOutput, calls=%fused_computation.3 | convolution fusion | flops 3221225472 | bytes 17563648 | tf_op jit(solution)/shard_map/dot_general | solution.py:89
  117.6 0.0 reduce-scatter.2.cloned.1.call-update
  117.6 96.8 %reduce-scatter.2.cloned.1.call-done = f32[512,256]{0,1:T(8,128)} async-done(((f32[4096,256]{0,1:T(8,128)}), f32[512,256]{0,1:T(8,128)}) %reduce-scatter.2.cloned.1.call-update) | async-done | bytes 524304 | tf_op jit(solution)/shard_map/reduce_scatter | solution.py:88
  214.4 1.1 fusion.33
  215.6 0.7 collective-permute-start
  216.2 6.7 %collective-permute-done = bf16[1,2,128,512]{3,2,1,0:T(8,128)(2,1)S(1)} collective-permute-done((bf16[1,2,128,512]{3,2,1,0:T(8,128)(2,1)S(1)}, bf16[1,2,128,512]{3,2,1,0:T(8,128)(2,1)S(1)}, u32[]{:S(2)}, u32[]{:S(2)}) %collective-permute-start) | collective-permute-done | bytes 262176 | tf_op jit(solution)/shard_map/ppermute | solution.py:10
  222.9 0.7 copy.114
  (20 shorter events, 0.2 us)
Async XLA Ops:
  6.5 77.9 %all-gather.2.cloned.1.call-start = ((), (), s32[]{:S(2)}) async-start(), calls=%async_computation.1 | async-start | bytes 2359296 | tf_op jit(solution)/shard_map/all_gather | solution.py:61
  7.3 17.0 %copy-start.4 = (f32[1,7,3,512]{3,0,2,1:T(1,128)S(1)}, f32[1,7,3,512]{3,0,2,1:T(1,128)}, u32[]{:S(2)}) copy-start(f32[1,7,3,512]{3,0,2,1:T(1,128)} %param.9) | copy-start | bytes 129028
  7.3 17.1 %copy-start.5 = (f32[1,128,32]{1,2,0:T(8,128)S(1)}, f32[1,128,32]{1,2,0:T(8,128)}, u32[]{:S(2)}) copy-start(f32[1,128,32]{1,2,0:T(8,128)} %param.10) | copy-start | bytes 49156
  7.3 207.2 %reduce-scatter.2.cloned.1.call-start = ((), (), s32[]{:S(2)}) async-start(), calls=%async_computation.2 | async-start | bytes 4718592 | tf_op jit(solution)/shard_map/reduce_scatter | solution.py:88
  92.6 2.5 %copy-start.2 = (bf16[1,2,128,512]{3,2,1,0:T(8,128)(2,1)S(1)}, bf16[1,2,128,512]{3,2,1,0:T(8,128)(2,1)}, u32[]{:S(2)}) copy-start(bf16[1,2,128,512]{3,2,1,0:T(8,128)(2,1)} %param.7) | copy-start | bytes 786436
  93.9 1.2 copy-start
  103.9 1.4 copy-start.1
  103.9 1.5 copy-start.3
  104.0 1.5 copy-start.6
  215.6 7.4 %collective-permute-start = (bf16[1,2,128,512]{3,2,1,0:T(8,128)(2,1)S(1)}, bf16[1,2,128,512]{3,2,1,0:T(8,128)(2,1)S(1)}, u32[]{:S(2)}, u32[]{:S(2)}) collective-permute-start(bf16[1,2,128,512]{3,2,1,0:T(8,128)(2,1)S(1)} %fusion.33), channel_id=1, source_target_pairs={{0,248},{8,0},{16,8},{24,16},{32,24},{40,32},{48,40},{56,48},{64,5... | collective-permute-start | bytes 786440 | tf_op jit(solution)/shard_map/ppermute | solution.py:10
Sparse Core Ops, SparseCore 0:
  9.1 56.8 all-gather.1
  117.7 96.6 reduce-scatter.1
where the time goes:
time: 232 us; the launch traced here: 230 us
  waiting for transfers between devices  104 us (45%)
  local copies, waits for them, and re-layouts  84.4 us (36%)
  matrix products  22.2 us (10%)
  between operations  13.6 us (6%)
  other arithmetic  5.22 us (2%)
    reduce_scatter x1, waiting for transfers between devices, section_backward(): lax.psum_scatter(lax.dot_general(slab_rows, conv_flat, (((1,), (1,)), (()...  96.8 us
    gather x2, local copies, waits for them, and re-layouts, toeplitz_of(): looked = jnp.take(medium.T, lag_index, axis=1)  59.9 us
    unnamed x21, local copies, waits for them, and re-layouts  20.3 us
    dot_general x1, matrix products, section_backward(): lax.dot_general(slab_rows, conv_flat, (((1,), (1,)), ((), ())), preferred...  9.74 us
    dot_general x1, matrix products, section_backward(): jnp.dot(flattened, slab_rows, preferred_element_type=jnp.float32)  7.15 us
    ppermute x1, waiting for transfers between devices, shifted(): return lax.ppermute(value, axis, pairs)  6.7 us
  transfers between devices with their start and end apart: 3, of which 2 were waited for; matrix products, arithmetic and copies ran while one was open for 33% of the time, Pallas kernels for 0%

commit v1 on v0

v1 whole, which is shorter than its diff:
```python
import functools

import jax
import jax.numpy as jnp
from jax import lax
from jax.experimental import pallas as pl
from jax.experimental.pallas import tpu as pltpu
from jax.sharding import PartitionSpec as P

MESH = pl.DeviceIdType.MESH
F32 = jnp.float32
BF16 = jnp.bfloat16
PAD = 8


def split_two(value):
    high = value.astype(BF16)
    low = (value - high.astype(F32)).astype(BF16)
    return high, low


def peer_of(me, offset, sign):
    column = lax.rem(lax.div(me, 2) + 4 + sign * (offset // 2 if isinstance(offset, int) else lax.div(offset, 2)), 4)
    row = lax.rem(me + (offset % 2 if isinstance(offset, int) else lax.rem(offset, 2)), 2)
    return column * 2 + row


def kernel(
    sections, x_hbm, inc_hbm, w_hbm, taps_hbm, medium_hbm, skip_hbm, out_hbm,
    xbuf, inc, w, taps, medium, flipped, skip, proj, turn, grad, fwd_t, bwd_t, own, sendbuf, recvbuf, final,
    local_sem, w_sem, ag_send, ag_recv, rs_send, rs_recv, fin_send, fin_recv,
):
    me = lax.axis_index("tp")
    sec = lax.axis_index("section")
    below = lax.rem(sec + sections - 1, sections)
    above = lax.rem(sec + 1, sections)
    micro, length, width = inc.shape
    blocks = width // 128

    def rows_of(device):
        return pl.ds(pl.multiple_of(device * width, width), width)

    small = [
        pltpu.make_async_copy(x_hbm.at[0], xbuf.at[:, 0], local_sem.at[0]),
        pltpu.make_async_copy(medium_hbm.at[0], medium, local_sem.at[1]),
        pltpu.make_async_copy(taps_hbm, taps, local_sem.at[2]),
        pltpu.make_async_copy(skip_hbm, skip, local_sem.at[3]),
        pltpu.make_async_copy(inc_hbm.at[0], inc, local_sem.at[4]),
    ]
    for copy in small[:2]:
        copy.start()

    def w_copy(offset):
        rows = rows_of(peer_of(me, offset, -1))
        return pltpu.make_async_copy(w_hbm.at[0, :, rows, :], w.at[:, rows, :], w_sem.at[offset])

    for offset in range(8):
        w_copy(offset).start()
    for copy in small[2:]:
        copy.start()

    barrier = pltpu.get_barrier_semaphore()
    for offset in range(1, 8):
        pl.semaphore_signal(barrier, inc=1, device_id={"tp": peer_of(me, offset, 1)}, device_id_type=MESH)
    pl.semaphore_signal(barrier, inc=1, device_id={"section": below}, device_id_type=MESH)
    pl.semaphore_signal(barrier, inc=1, device_id={"section": above}, device_id_type=MESH)
    pl.semaphore_wait(barrier, 9)

    def ag_copy(mb, offset):
        return pltpu.make_async_remote_copy(
            src_ref=x_hbm.at[0, mb],
            dst_ref=xbuf.at[mb, offset],
            send_sem=ag_send.at[mb, offset],
            recv_sem=ag_recv.at[mb, offset],
            device_id={"tp": peer_of(me, offset, 1)},
            device_id_type=MESH,
        )

    for mb in range(micro):
        for offset in (1, 2, 6, 3, 7, 4, 5):
            ag_copy(mb, offset).start()

    small[1].wait()
    place_r = lax.broadcasted_iota(jnp.int32, (128, 128), 0)
    place_c = lax.broadcasted_iota(jnp.int32, (128, 128), 1)
    flip = jnp.where(lax.rem(place_r + place_c, 128) == 0, 1.0, 0.0).astype(F32)
    backward = jnp.dot(medium[...], flip, precision=lax.Precision.HIGHEST, preferred_element_type=F32)
    flipped[...] = backward

    def build(group, carry):
        rows = pl.ds(pl.multiple_of(group * 128, 128), 128)
        ahead = jnp.broadcast_to(medium[pl.ds(group, 1), :], (128, 128))
        ahead = pltpu.roll(ahead, 0, 1, stride=1, stride_axis=0)
        high, low = split_two(jnp.where(place_c >= place_r, ahead, 0.0))
        bwd_t[rows, 0:128] = high
        bwd_t[rows, 128:256] = low
        behind = jnp.broadcast_to(flipped[pl.ds(group, 1), :], (128, 128))
        behind = pltpu.roll(behind, 0, 1, stride=1, stride_axis=0)
        high, low = split_two(jnp.where(place_c <= place_r, behind, 0.0))
        fwd_t[rows, 0:128] = high
        fwd_t[rows, 128:256] = low
        return carry

    lax.fori_loop(0, 32, build, 0)

    for part in range(3 * blocks):
        proj[part, 0:PAD, :] = jnp.zeros((PAD, 128), F32)
        turn[part, length : length + PAD, :] = jnp.zeros((PAD, 128), F32)
    for copy in small[2:]:
        copy.wait()
    small[0].wait()

    def gathered(mb, offset, first):
        rows = rows_of(peer_of(me, offset, -1))
        chunk = xbuf[mb, offset]
        for stream in range(3):
            part = jnp.dot(chunk, w[stream, rows, :], preferred_element_type=F32)
            for block in range(blocks):
                piece = part[:, block * 128 : block * 128 + 128]
                where = (stream * blocks + block, pl.ds(PAD, length), slice(None))
                proj[where] = piece if first else proj[where] + piece

    def medium_conv(table, block, value):
        high, low = split_two(value)
        both = jnp.concatenate([high, low], axis=1)
        both = jnp.concatenate([both, both], axis=0)
        rows = pl.ds(pl.multiple_of(block * 1024, 1024), 1024)
        raw = jnp.dot(table[rows, :], both, preferred_element_type=F32)
        lane_group = lax.div(lax.broadcasted_iota(jnp.int32, (length, 128), 1), 16)
        total = raw[0:length, 0:128] + raw[0:length, 128:256]
        for group in range(1, 8):
            first = group * 128
            piece = raw[first : first + length, 0:128] + raw[first : first + length, 128:256]
            total = jnp.where(lane_group == group, piece, total)
        return total

    def mixer(mb):
        def one_block(block, carry):
            lanes = pl.ds(pl.multiple_of(block * 128, 128), 128)

            def featured(stream):
                total = jnp.zeros((length, 128), F32)
                for lag in range(7):
                    tap = taps[lag * 3 + stream, :, lanes]
                    total = total + tap * proj[stream * blocks + block, pl.ds(PAD - lag, length), :]
                return total

            query, key, value = featured(0), featured(1), featured(2)
            gain = skip[:, lanes]
            product = key * value
            mixed = medium_conv(fwd_t, block, product) + gain * product
            upstream = inc[mb, :, lanes].astype(F32)
            mixed_grad = upstream * query
            product_grad = medium_conv(bwd_t, block, mixed_grad) + gain * mixed_grad
            turn[block, 0:length, :] = upstream * mixed
            turn[blocks + block, 0:length, :] = product_grad * value
            turn[2 * blocks + block, 0:length, :] = product_grad * key
            for stream in range(3):
                total = jnp.zeros((length, 128), F32)
                for lag in range(7):
                    tap = taps[lag * 3 + stream, :, lanes]
                    total = total + tap * turn[stream * blocks + block, pl.ds(lag, length), :]
                grad[stream, :, lanes] = total.astype(BF16)
            return carry

        lax.fori_loop(0, blocks, one_block, 0)

    def share(offset):
        rows = rows_of(peer_of(me, offset, 1))
        total = None
        for stream in range(3):
            part = lax.dot_general(
                grad[stream], w[stream, rows, :], (((1,), (1,)), ((), ())), preferred_element_type=F32
            )
            total = part if total is None else total + part
        return total

    def rs_copy(mb, offset):
        return pltpu.make_async_remote_copy(
            src_ref=sendbuf.at[mb, offset - 1],
            dst_ref=recvbuf.at[mb, offset - 1],
            send_sem=rs_send.at[mb, offset],
            recv_sem=rs_recv.at[mb, offset],
            device_id={"tp": peer_of(me, offset, 1)},
            device_id_type=MESH,
        )

    for mb in range(micro):
        if mb == 0:
            w_copy(0).wait()
        gathered(mb, 0, True)

        def step(offset, carry, mb=mb):
            if mb == 0:
                w_copy(offset).wait()
            ag_copy(mb, offset).wait_recv()
            gathered(mb, offset, False)
            return carry

        lax.fori_loop(1, 8, step, 0)
        mixer(mb)

        def push(offset, carry, mb=mb):
            sendbuf[mb, offset - 1] = share(offset).astype(BF16)
            rs_copy(mb, offset).start()
            return carry

        lax.fori_loop(1, 8, push, 0)
        own[mb] = share(0) + inc[mb].astype(F32)

    def fin_copy(mb):
        return pltpu.make_async_remote_copy(
            src_ref=final.at[mb],
            dst_ref=out_hbm.at[0, mb],
            send_sem=fin_send.at[mb],
            recv_sem=fin_recv.at[mb],
            device_id={"section": below},
            device_id_type=MESH,
        )

    for mb in range(micro):
        def collect(offset, carry, mb=mb):
            rs_copy(mb, offset).wait_recv()
            own[mb] = own[mb] + recvbuf[mb, offset - 1].astype(F32)
            return carry

        lax.fori_loop(1, 8, collect, 0)
        final[mb] = own[mb].astype(BF16)
        fin_copy(mb).start()

    for mb in range(micro):
        def drain(offset, carry, mb=mb):
            ag_copy(mb, offset).wait_send()
            rs_copy(mb, offset).wait_send()
            return carry

        lax.fori_loop(1, 8, drain, 0)
    for mb in range(micro):
        fin_copy(mb).wait()


def local(sections, block_input, incoming, in_weight, short_taps, medium_taps, skip_weight):
    _, micro, length, width = block_input.shape
    model_width = in_weight.shape[1]
    lags = short_taps.shape[1]
    groups = medium_taps.shape[2]
    weights = jnp.transpose(in_weight, (0, 2, 1, 3))
    taps = jnp.transpose(short_taps, (1, 2, 0, 3)).reshape(lags * 3, 1, width)
    medium = jnp.transpose(medium_taps, (0, 2, 1))
    parts = 3 * (width // 128)
    anywhere = pl.BlockSpec(memory_space=pl.ANY)
    dma = pltpu.SemaphoreType.DMA
    return pl.pallas_call(
        functools.partial(kernel, sections),
        out_shape=jax.ShapeDtypeStruct(block_input.shape, BF16),
        in_specs=[anywhere] * 6,
        out_specs=anywhere,
        scratch_shapes=[
            pltpu.VMEM((micro, 8, length, width), BF16),
            pltpu.VMEM((micro, length, width), BF16),
            pltpu.VMEM((3, model_width, width), BF16),
            pltpu.VMEM((lags * 3, 1, width), F32),
            pltpu.VMEM((groups, 128), F32),
            pltpu.VMEM((groups, 128), F32),
            pltpu.VMEM((1, width), F32),
            pltpu.VMEM((parts, length + PAD, 128), F32),
            pltpu.VMEM((parts, length + PAD, 128), F32),
            pltpu.VMEM((3, length, width), BF16),
            pltpu.VMEM((groups * 128, 256), BF16),
            pltpu.VMEM((groups * 128, 256), BF16),
            pltpu.VMEM((micro, length, width), F32),
            pltpu.VMEM((micro, 7, length, width), BF16),
            pltpu.VMEM((micro, 7, length, width), BF16),
            pltpu.VMEM((micro, length, width), BF16),
            dma((5,)),
            dma((8,)),
            dma((micro, 8)),
            dma((micro, 8)),
            dma((micro, 8)),
            dma((micro, 8)),
            dma((micro,)),
            dma((micro,)),
        ],
        compiler_params=pltpu.CompilerParams(
            collective_id=0, has_side_effects=True, vmem_limit_bytes=56 * 1024 * 1024
        ),
    )(block_input, incoming, weights, taps, medium, skip_weight)


def solution(mesh):
    in_specs = (
        P("section", None, None, "tp"),
        P("section", None, None, "tp"),
        P("section", None, None, "tp"),
        P("section", None, None, "tp"),
        P("section", None, "tp"),
        P("section", "tp"),
    )
    out_specs = P("section", None, None, "tp")
    return jax.shard_map(
        functools.partial(local, mesh.shape["section"]),
        mesh=mesh, in_specs=in_specs, out_specs=out_specs, check_vma=False,
    )
```

time: 232 us -> 67.1 us (0.29)
  waiting for transfers between devices: 104 us -> 0 us
  local copies, waits for them, and re-layouts: 84.4 us -> 1.67 us
  Pallas kernels: 0 us -> 64.3 us
  matrix products: 22.2 us -> 0 us
  between operations: 13.6 us -> 0.01 us
  other arithmetic: 5.22 us -> 0 us
    reduce_scatter x1 -> x0, waiting for transfers between devices: 96.8 us -> none  [section_backward(): lax.psum_scatter(lax.dot_general(slab_rows, conv_flat, (((1,), (1,)), (()...]
    pallas_call x0 -> x1, Pallas kernels: none -> 64.3 us  [local(): pl.pallas_call(functools.partial(kernel, sections), out_shape=jax.ShapeDt...]
    gather x2 -> x0, local copies, waits for them, and re-layouts: 59.9 us -> none  [toeplitz_of(): looked = jnp.take(medium.T, lag_index, axis=1)]
    dot_general x4 -> x0, matrix products: 22.2 us -> none  [the longest x1 9.74 us: section_backward(): lax.dot_general(slab_rows, conv_flat, (((1,), (1,)), ((), ())), preferred...]
    unnamed x21 -> x1, local copies, waits for them, and re-layouts: 20.3 us -> 1.67 us
    ppermute x1 -> x0, waiting for transfers between devices: 6.7 us -> none  [shifted(): return lax.ppermute(value, axis, pairs)]
    convert_element_type x2 -> x0, other arithmetic: 2.42 us -> none  [the longest x1 1.31 us: section_backward(): conv_grad = anti_taps(stream_grad, short_taps).astype(jnp.bfloat16)]
  transfers between devices with their start and end apart: 3 -> 0, of which waited for: 2 -> 0; matrix products, arithmetic and copies ran while one was open for 33% -> 0% of each run, Pallas kernels for 0% -> 0%
where the time goes in v1:
time: 67.1 us; the launch traced here: 66 us
  Pallas kernels  64.3 us (96%)
  local copies, waits for them, and re-layouts  1.67 us (2%)
    pallas_call x1, Pallas kernels, local(): pl.pallas_call(functools.partial(kernel, sections), out_shape=jax.ShapeDt...  64.3 us
    unnamed x1, local copies, waits for them, and re-layouts  1.67 us

profile of v1, /device:TPU:1, one launch (start us, length us, event | category | flops | bytes accessed | tf_op | source)
XLA Modules:
  0.0 66.0 jit_solution(6342648724866872847)
XLA Ops:
  0.0 64.3 %shard_map.64 = bf16[1,2,128,512]{3,2,1,0:T(8,128)(2,1)} custom-call(bf16[1,2,128,512]{3,2,1,0:T(8,128)(2,1)} %x_hbm.1, bf16[1,2,128,512]{3,2,1,0:T(8,128)(2,1)} %inc_hbm.1, bf16[1,3,4096,512]{3,2,1,0:T(8,128)(2,1)} %bitcast.3, f32[21,1,512]{2,1,0:T(1,128)} %bitcast.4, f32[1,32,128]{2,1,0:T(8,128)} %bitcast.5, f32[1,512]{1,0:T(1,128)} %skip_hbm.1), custom_call_target="tpu_custom_call" | custom-call | tf_op jit(solution)/shard_map/pallas_call | solution.py:253
  64.3 1.7 %copy.8 = bf16[1,2,128,512]{3,2,1,0:T(8,128)(2,1)} copy(bf16[1,2,128,512]{3,2,1,0:T(8,128)(2,1)} %shard_map.64) | data formatting | bytes 524288

commit v2 on v1

v2 whole, which is shorter than its diff:
```python
import functools

import jax
import jax.numpy as jnp
from jax import lax
from jax.experimental import pallas as pl
from jax.experimental.pallas import tpu as pltpu
from jax.sharding import PartitionSpec as P

MESH = pl.DeviceIdType.MESH
F32 = jnp.float32
BF16 = jnp.bfloat16
PAD = 8
HALF = 256
RIGHT, LEFT, ACROSS = (1, 0), (3, 0), (0, 1)

ORIGIN = {
    0: [(RIGHT, (1, 0)), (LEFT, (3, 0)), (ACROSS, (0, 1))],
    1: [(ACROSS, (0, 1)), (RIGHT, (1, 0)), (LEFT, (3, 0))],
}


def forwards(mb, cls, key):
    if cls == 0:
        far = RIGHT if mb == 0 else LEFT
        table = {
            (1, 0): [(ACROSS, (1, 1))],
            (3, 0): [(ACROSS, (3, 1))],
            (2, 0): [(ACROSS, (2, 1))],
        }
        table[far].insert(0, (far, (2, 0)))
    else:
        table = {
            (0, 1): [(RIGHT, (1, 1)), (LEFT, (3, 1))],
            (1, 0): [(RIGHT, (2, 0))],
            (3, 1): [(LEFT, (2, 1))],
        }
    return table.get(key, [])


def returns(mb, cls, key):
    if cls == 0:
        far = RIGHT if mb == 0 else LEFT
        if key[1] == 1:
            return ACROSS, []
        if key == (2, 0):
            return far, [(2, 1)]
        if key == (0, 0):
            return None, [(0, 1), (1, 0), (3, 0)]
        return key, [(key[0], 1)] + ([(2, 0)] if key == far else [])
    return {
        (2, 0): (RIGHT, []),
        (2, 1): (LEFT, []),
        (1, 1): (RIGHT, []),
        (3, 0): (LEFT, []),
        (1, 0): (RIGHT, [(2, 0)]),
        (3, 1): (LEFT, [(2, 1)]),
        (0, 1): (ACROSS, [(1, 1), (3, 1)]),
        (0, 0): (None, [(3, 0), (1, 0), (0, 1)]),
    }[key]


def slot(key):
    return key[0] * 2 + key[1]


def split_two(value):
    high = value.astype(BF16)
    low = (value - high.astype(F32)).astype(BF16)
    return high, low


def kernel(
    sections, x_hbm, inc_hbm, w_hbm, taps_hbm, medium_hbm, skip_hbm, out_hbm,
    xbuf, inc, w, taps, medium, flipped, skip, proj, turn, grad_t, fwd_t, bwd_t, partial, sendbuf, recvbuf, final,
    local_sem, w_sem, ag_send, ag_recv, rs_send, rs_recv, fin_send, fin_recv,
):
    me = lax.axis_index("tp")
    sec = lax.axis_index("section")
    below = lax.rem(sec + sections - 1, sections)
    above = lax.rem(sec + 1, sections)
    micro, length, width = inc.shape
    blocks = width // 128
    column, row = lax.div(me, 2), lax.rem(me, 2)

    def device_at(dx, dy):
        return lax.rem(column + 4 + dx, 4) * 2 + lax.rem(row + dy, 2)

    def rows_of(device, start, size):
        return pl.ds(pl.multiple_of(device * width + start, HALF), size)

    small = [
        pltpu.make_async_copy(medium_hbm.at[0], medium, local_sem.at[0]),
        pltpu.make_async_copy(taps_hbm, taps, local_sem.at[1]),
        pltpu.make_async_copy(skip_hbm, skip, local_sem.at[2]),
        pltpu.make_async_copy(inc_hbm.at[0], inc, local_sem.at[3]),
    ]
    own_x = [
        [
            pltpu.make_async_copy(
                x_hbm.at[0, mb, :, pl.ds(cls * HALF, HALF)], xbuf.at[mb, cls, 0], local_sem.at[4 + mb * 2 + cls]
            )
            for cls in range(2)
        ]
        for mb in range(micro)
    ]

    def w_copy(key):
        rows = rows_of(device_at(-key[0], key[1]), 0, width)
        return pltpu.make_async_copy(w_hbm.at[0, :, rows, :], w.at[:, rows, :], w_sem.at[slot(key)])

    barrier = pltpu.get_barrier_semaphore()
    for hop in (RIGHT, LEFT, ACROSS):
        pl.semaphore_signal(barrier, inc=1, device_id={"tp": device_at(*hop)}, device_id_type=MESH)
    pl.semaphore_signal(barrier, inc=1, device_id={"section": below}, device_id_type=MESH)
    pl.semaphore_signal(barrier, inc=1, device_id={"section": above}, device_id_type=MESH)
    for mb in range(micro):
        for cls in range(2):
            own_x[mb][cls].start()
    small[0].start()
    arrival = [(0, 0), (0, 1), (1, 0), (3, 0), (3, 1), (2, 0), (1, 1), (2, 1)]
    for key in arrival:
        w_copy(key).start()
    for copy in small[1:]:
        copy.start()

    place_r = lax.broadcasted_iota(jnp.int32, (128, 128), 0)
    place_c = lax.broadcasted_iota(jnp.int32, (128, 128), 1)
    small[0].wait()
    flip = jnp.where(lax.rem(place_r + place_c, 128) == 0, 1.0, 0.0).astype(F32)
    flipped[...] = jnp.dot(medium[...], flip, precision=lax.Precision.HIGHEST, preferred_element_type=F32)
    for part in range(3 * blocks):
        proj[part, 0:PAD, :] = jnp.zeros((PAD, 128), F32)
        turn[part, length : length + PAD, :] = jnp.zeros((PAD, 128), F32)
    for mb in range(micro):
        for cls in range(2):
            own_x[mb][cls].wait()

    pl.semaphore_wait(barrier, 5)

    sent = []

    def gather_copy(mb, cls, source, hop, key):
        return pltpu.make_async_remote_copy(
            src_ref=xbuf.at[mb, cls, slot(source)],
            dst_ref=xbuf.at[mb, cls, slot(key)],
            send_sem=ag_send.at[mb, cls, slot(key)],
            recv_sem=ag_recv.at[mb, cls, slot(key)],
            device_id={"tp": device_at(*hop)},
            device_id_type=MESH,
        )

    def gather_start(mb):
        for cls in (1, 0):
            for hop, key in ORIGIN[cls]:
                copy = gather_copy(mb, cls, (0, 0), hop, key)
                copy.start()
                sent.append(copy)

    def gather_handle(mb, *units):
        for cls, key in units:
            gather_copy(mb, cls, (0, 0), RIGHT, key).wait_recv()
            for hop, there in forwards(mb, cls, key):
                copy = gather_copy(mb, cls, key, hop, there)
                copy.start()
                sent.append(copy)

    def project(mb, units, first=False):
        for stream in range(3):
            total = None
            for cls, key in units:
                rows = rows_of(device_at(-key[0], key[1]), cls * HALF, HALF)
                part = jnp.dot(xbuf[mb, cls, slot(key)], w[stream, rows, :], preferred_element_type=F32)
                total = part if total is None else total + part
            for block in range(blocks):
                piece = total[:, block * 128 : block * 128 + 128]
                where = (stream * blocks + block, pl.ds(PAD, length), slice(None))
                proj[where] = piece if first else proj[where] + piece

    def build_tables(begin, end):
        def build(group, carry):
            rows = pl.ds(pl.multiple_of(group * 128, 128), 128)
            ahead = jnp.broadcast_to(medium[pl.ds(group, 1), :], (128, 128))
            ahead = pltpu.roll(ahead, 0, 1, stride=1, stride_axis=0)
            high, low = split_two(jnp.where(place_c >= place_r, ahead, 0.0))
            bwd_t[rows, 0:128] = high
            bwd_t[rows, 128:256] = low
            behind = jnp.broadcast_to(flipped[pl.ds(group, 1), :], (128, 128))
            behind = pltpu.roll(behind, 0, 1, stride=1, stride_axis=0)
            high, low = split_two(jnp.where(place_c <= place_r, behind, 0.0))
            fwd_t[rows, 0:128] = high
            fwd_t[rows, 128:256] = low
            return carry

        lax.fori_loop(begin, end, build, 0)

    def medium_conv(table, block, value):
        high, low = split_two(value)
        both = jnp.concatenate([high, low], axis=1)
        both = jnp.concatenate([both, both], axis=0)
        rows = pl.ds(pl.multiple_of(block * 1024, 1024), 1024)
        raw = jnp.dot(table[rows, :], both, preferred_element_type=F32)
        lane_group = lax.div(place_c, 16)
        total = raw[0:length, 0:128] + raw[0:length, 128:256]
        for group in range(1, 8):
            first = group * 128
            piece = raw[first : first + length, 0:128] + raw[first : first + length, 128:256]
            total = jnp.where(lane_group == group, piece, total)
        return total

    def mixer(mb, begin, end):
        def one_block(block, carry):
            lanes = pl.ds(pl.multiple_of(block * 128, 128), 128)

            def featured(stream):
                total = jnp.zeros((length, 128), F32)
                for lag in range(7):
                    tap = taps[lag * 3 + stream, :, lanes]
                    total = total + tap * proj[stream * blocks + block, pl.ds(PAD - lag, length), :]
                return total

            query, key, value = featured(0), featured(1), featured(2)
            gain = skip[:, lanes]
            product = key * value
            mixed = medium_conv(fwd_t, block, product) + gain * product
            upstream = inc[mb, :, lanes].astype(F32)
            mixed_grad = upstream * query
            product_grad = medium_conv(bwd_t, block, mixed_grad) + gain * mixed_grad
            turn[block, 0:length, :] = upstream * mixed
            turn[blocks + block, 0:length, :] = product_grad * value
            turn[2 * blocks + block, 0:length, :] = product_grad * key
            for stream in range(3):
                total = jnp.zeros((length, 128), F32)
                for lag in range(7):
                    tap = taps[lag * 3 + stream, :, lanes]
                    total = total + tap * turn[stream * blocks + block, pl.ds(lag, length), :]
                rows = pl.ds(pl.multiple_of(stream * width + block * 128, 128), 128)
                grad_t[rows, :] = jnp.transpose(total).astype(BF16)
            return carry

        lax.fori_loop(begin, end, one_block, 0)

    def sum_copy(mb, cls, key, hop):
        return pltpu.make_async_remote_copy(
            src_ref=sendbuf.at[mb, cls, slot(key)],
            dst_ref=recvbuf.at[mb, cls, slot(key)],
            send_sem=rs_send.at[mb, cls, slot(key)],
            recv_sem=rs_recv.at[mb, cls, slot(key)],
            device_id={"tp": device_at(*hop)},
            device_id_type=MESH,
        )

    def push_sum(mb, cls, key, hop, value):
        sendbuf[mb, cls, slot(key)] = value.astype(BF16)
        copy = sum_copy(mb, cls, key, hop)
        copy.start()
        sent.append(copy)

    def share(mb, *keys):
        for key in keys:
            rows = rows_of(device_at(*key), 0, width)
            total = None
            for stream in range(3):
                part = jnp.dot(
                    w[stream, rows, :], grad_t[stream * width : stream * width + width, :], preferred_element_type=F32
                )
                total = part if total is None else total + part
            for cls in range(2):
                piece = total[cls * HALF : cls * HALF + HALF, :]
                hop, joins = returns(mb, cls, key)
                if hop is not None and not joins:
                    push_sum(mb, cls, key, hop, piece)
                else:
                    partial[cls, slot(key)] = piece

    def combine(mb, cls, key):
        hop, joins = returns(mb, cls, key)
        total = partial[cls, slot(key)]
        for join in joins:
            sum_copy(mb, cls, join, RIGHT).wait_recv()
            total = total + recvbuf[mb, cls, slot(join)].astype(F32)
        if hop is not None:
            push_sum(mb, cls, key, hop, total)
            return
        upstream = inc[mb, :, cls * HALF : cls * HALF + HALF].astype(F32)
        final[mb, cls] = (jnp.transpose(total) + upstream).astype(BF16)
        copy = pltpu.make_async_remote_copy(
            src_ref=final.at[mb, cls],
            dst_ref=out_hbm.at[0, mb, :, pl.ds(cls * HALF, HALF)],
            send_sem=fin_send.at[mb, cls],
            recv_sem=fin_recv.at[mb, cls],
            device_id={"section": below},
            device_id_type=MESH,
        )
        copy.start()
        ended.append(copy)

    ended = []
    group_a = [(1, (0, 1)), (0, (1, 0)), (0, (3, 0)), (1, (1, 0))]
    group_b = [(1, (3, 1)), (0, (2, 0))]
    group_c = [(1, (3, 0)), (0, (0, 1))]
    group_d = [(1, (1, 1)), (0, (1, 1)), (0, (3, 1)), (1, (2, 0))]
    group_e = [(1, (2, 1)), (0, (2, 1))]
    owned = [(0, (0, 0)), (1, (0, 0))]

    gather_start(0)
    build_tables(0, 12)
    w_copy((0, 0)).wait()
    project(0, owned, first=True)
    gather_handle(0, *group_a)
    gather_start(1)
    for key in arrival[1:]:
        w_copy(key).wait()
    project(0, group_a)
    gather_handle(0, *group_b)
    build_tables(12, 22)
    gather_handle(0, *group_c)
    project(0, group_b + group_c)
    build_tables(22, 32)
    gather_handle(0, *group_d)
    project(0, group_d)
    gather_handle(1, *group_a)
    gather_handle(0, *group_e)
    project(0, group_e)
    for copy in small[1:]:
        copy.wait()
    mixer(0, 0, 2)
    gather_handle(1, *group_b)
    mixer(0, 2, 4)
    share(0, (2, 1), (2, 0), (1, 1), (3, 1), (0, 1), (3, 0), (1, 0), (0, 0))
    project(1, owned, first=True)
    project(1, group_a)
    combine(0, 0, (2, 0))
    combine(0, 1, (1, 0))
    combine(0, 1, (3, 1))
    gather_handle(1, *group_c)
    project(1, group_b + group_c)
    combine(0, 0, (3, 0))
    combine(0, 0, (1, 0))
    combine(0, 1, (0, 1))
    gather_handle(1, *group_d)
    project(1, group_d)
    gather_handle(1, *group_e)
    project(1, group_e)
    mixer(1, 0, 2)
    combine(0, 0, (0, 0))
    combine(0, 1, (0, 0))
    mixer(1, 2, 4)
    share(1, (2, 1), (2, 0), (1, 1), (3, 1))
    combine(1, 0, (2, 0))
    combine(1, 1, (3, 1))
    share(1, (0, 1), (3, 0), (1, 0))
    combine(1, 1, (1, 0))
    combine(1, 0, (1, 0))
    combine(1, 0, (3, 0))
    combine(1, 1, (0, 1))
    share(1, (0, 0))
    combine(1, 0, (0, 0))
    combine(1, 1, (0, 0))
    for copy in sent:
        copy.wait_send()
    for copy in ended:
        copy.wait()


def local(sections, block_input, incoming, in_weight, short_taps, medium_taps, skip_weight):
    _, micro, length, width = block_input.shape
    model_width = in_weight.shape[1]
    lags = short_taps.shape[1]
    groups = medium_taps.shape[2]
    weights = jnp.transpose(in_weight, (0, 2, 1, 3))
    taps = jnp.transpose(short_taps, (1, 2, 0, 3)).reshape(lags * 3, 1, width)
    medium = jnp.transpose(medium_taps, (0, 2, 1))
    parts = 3 * (width // 128)
    anywhere = pl.BlockSpec(memory_space=pl.ANY)
    dma = pltpu.SemaphoreType.DMA
    return pl.pallas_call(
        functools.partial(kernel, sections),
        out_shape=jax.ShapeDtypeStruct(block_input.shape, BF16),
        in_specs=[anywhere] * 6,
        out_specs=anywhere,
        scratch_shapes=[
            pltpu.VMEM((micro, 2, 8, length, HALF), BF16),
            pltpu.VMEM((micro, length, width), BF16),
            pltpu.VMEM((3, model_width, width), BF16),
            pltpu.VMEM((lags * 3, 1, width), F32),
            pltpu.VMEM((groups, 128), F32),
            pltpu.VMEM((groups, 128), F32),
            pltpu.VMEM((1, width), F32),
            pltpu.VMEM((parts, length + PAD, 128), F32),
            pltpu.VMEM((parts, length + PAD, 128), F32),
            pltpu.VMEM((3 * width, length), BF16),
            pltpu.VMEM((groups * 128, 256), BF16),
            pltpu.VMEM((groups * 128, 256), BF16),
            pltpu.VMEM((2, 8, HALF, length), F32),
            pltpu.VMEM((micro, 2, 8, HALF, length), BF16),
            pltpu.VMEM((micro, 2, 8, HALF, length), BF16),
            pltpu.VMEM((micro, 2, length, HALF), BF16),
            dma((8,)),
            dma((8,)),
            dma((micro, 2, 8)),
            dma((micro, 2, 8)),
            dma((micro, 2, 8)),
            dma((micro, 2, 8)),
            dma((micro, 2)),
            dma((micro, 2)),
        ],
        compiler_params=pltpu.CompilerParams(
            collective_id=0, has_side_effects=True, vmem_limit_bytes=56 * 1024 * 1024
        ),
    )(block_input, incoming, weights, taps, medium, skip_weight)


def solution(mesh):
    in_specs = (
        P("section", None, None, "tp"),
        P("section", None, None, "tp"),
        P("section", None, None, "tp"),
        P("section", None, None, "tp"),
        P("section", None, "tp"),
        P("section", "tp"),
    )
    out_specs = P("section", None, None, "tp")
    return jax.shard_map(
        functools.partial(local, mesh.shape["section"]),
        mesh=mesh, in_specs=in_specs, out_specs=out_specs, check_vma=False,
    )
```

time: 67.1 us -> 62.9 us (0.937)
  Pallas kernels: 64.3 us -> 60.7 us
    pallas_call x1, Pallas kernels: 64.3 us -> 60.7 us  [local(): pl.pallas_call(functools.partial(kernel, sections), out_shape=jax.ShapeDt...]
where the time goes in v2:
time: 62.9 us; the launch traced here: 62.4 us
  Pallas kernels  60.7 us (97%)
  local copies, waits for them, and re-layouts  1.67 us (3%)
    pallas_call x1, Pallas kernels, local(): pl.pallas_call(functools.partial(kernel, sections), out_shape=jax.ShapeDt...  60.7 us
    unnamed x1, local copies, waits for them, and re-layouts  1.67 us

profile of v2, /device:TPU:1, one launch (start us, length us, event | category | flops | bytes accessed | tf_op | source)
XLA Modules:
  0.0 62.4 jit_solution(10045344160670382980)
XLA Ops:
  0.0 60.7 %shard_map.64 = bf16[1,2,128,512]{3,2,1,0:T(8,128)(2,1)} custom-call(bf16[1,2,128,512]{3,2,1,0:T(8,128)(2,1)} %x_hbm.1, bf16[1,2,128,512]{3,2,1,0:T(8,128)(2,1)} %inc_hbm.1, bf16[1,3,4096,512]{3,2,1,0:T(8,128)(2,1)} %bitcast.3, f32[21,1,512]{2,1,0:T(1,128)} %bitcast.4, f32[1,32,128]{2,1,0:T(8,128)} %bitcast.5, f32[1,512]{1,0:T(1,128)} %skip_hbm.1), custom_call_target="tpu_custom_call" | custom-call | tf_op jit(solution)/shard_map/pallas_call | solution.py:377
  60.7 1.7 %copy.8 = bf16[1,2,128,512]{3,2,1,0:T(8,128)(2,1)} copy(bf16[1,2,128,512]{3,2,1,0:T(8,128)(2,1)} %shard_map.64) | data formatting | bytes 524288

commit v3 on v2

--- a/solution.py
+++ b/solution.py
@@ -118,7 +118,7 @@
         for cls in range(2):
             own_x[mb][cls].start()
     small[0].start()
-    arrival = [(0, 0), (0, 1), (1, 0), (3, 0), (3, 1), (2, 0), (1, 1), (2, 1)]
+    arrival = [(0, 0), (0, 1), (1, 0), (3, 0), (1, 1), (3, 1), (2, 0), (2, 1)]
     for key in arrival:
         w_copy(key).start()
     for copy in small[1:]:
@@ -130,7 +130,8 @@
     flip = jnp.where(lax.rem(place_r + place_c, 128) == 0, 1.0, 0.0).astype(F32)
     flipped[...] = jnp.dot(medium[...], flip, precision=lax.Precision.HIGHEST, preferred_element_type=F32)
     for part in range(3 * blocks):
-        proj[part, 0:PAD, :] = jnp.zeros((PAD, 128), F32)
+        for mb in range(micro):
+            proj[mb, part, 0:PAD, :] = jnp.zeros((PAD, 128), F32)
         turn[part, length : length + PAD, :] = jnp.zeros((PAD, 128), F32)
     for mb in range(micro):
         for cls in range(2):
@@ -150,34 +151,36 @@
             device_id_type=MESH,
         )
 
-    def gather_start(mb):
-        for cls in (1, 0):
-            for hop, key in ORIGIN[cls]:
-                copy = gather_copy(mb, cls, (0, 0), hop, key)
-                copy.start()
-                sent.append(copy)
-
-    def gather_handle(mb, *units):
-        for cls, key in units:
-            gather_copy(mb, cls, (0, 0), RIGHT, key).wait_recv()
-            for hop, there in forwards(mb, cls, key):
-                copy = gather_copy(mb, cls, key, hop, there)
-                copy.start()
-                sent.append(copy)
-
-    def project(mb, units, first=False):
+    def origin(mb, cls, number):
+        hop, key = ORIGIN[cls][number]
+        copy = gather_copy(mb, cls, (0, 0), hop, key)
+        copy.start()
+        sent.append(copy)
+
+    def handle(mb, cls, dx, dy):
+        gather_copy(mb, cls, (0, 0), RIGHT, (dx, dy)).wait_recv()
+        for hop, there in forwards(mb, cls, (dx, dy)):
+            copy = gather_copy(mb, cls, (dx, dy), hop, there)
+            copy.start()
+            sent.append(copy)
+
+    loaded, begun = set(), set()
+
+    def project(mb, dx, dy):
+        if (dx, dy) not in loaded:
+            w_copy((dx, dy)).wait()
+            loaded.add((dx, dy))
+        rows = rows_of(device_at(-dx, dy), 0, width)
+        chunk = jnp.concatenate([xbuf[mb, 0, slot((dx, dy))], xbuf[mb, 1, slot((dx, dy))]], axis=1)
         for stream in range(3):
-            total = None
-            for cls, key in units:
-                rows = rows_of(device_at(-key[0], key[1]), cls * HALF, HALF)
-                part = jnp.dot(xbuf[mb, cls, slot(key)], w[stream, rows, :], preferred_element_type=F32)
-                total = part if total is None else total + part
+            total = jnp.dot(chunk, w[stream, rows, :], preferred_element_type=F32)
             for block in range(blocks):
                 piece = total[:, block * 128 : block * 128 + 128]
-                where = (stream * blocks + block, pl.ds(PAD, length), slice(None))
-                proj[where] = piece if first else proj[where] + piece
-
-    def build_tables(begin, end):
+                where = (mb, stream * blocks + block, pl.ds(PAD, length), slice(None))
+                proj[where] = proj[where] + piece if mb in begun else piece
+        begun.add(mb)
+
+    def build_tables(number):
         def build(group, carry):
             rows = pl.ds(pl.multiple_of(group * 128, 128), 128)
             ahead = jnp.broadcast_to(medium[pl.ds(group, 1), :], (128, 128))
@@ -192,7 +195,7 @@
             fwd_t[rows, 128:256] = low
             return carry
 
-        lax.fori_loop(begin, end, build, 0)
+        lax.fori_loop(4 * number, 4 * number + 4, build, 0)
 
     def medium_conv(table, block, value):
         high, low = split_two(value)
@@ -208,7 +211,12 @@
             total = jnp.where(lane_group == group, piece, total)
         return total
 
-    def mixer(mb, begin, end):
+    ready = []
+
+    def mixer(mb, half):
+        while len(ready) < len(small) - 1:
+            ready.append(small[len(ready) + 1].wait())
+
         def one_block(block, carry):
             lanes = pl.ds(pl.multiple_of(block * 128, 128), 128)
 
@@ -216,7 +224,7 @@
                 total = jnp.zeros((length, 128), F32)
                 for lag in range(7):
                     tap = taps[lag * 3 + stream, :, lanes]
-                    total = total + tap * proj[stream * blocks + block, pl.ds(PAD - lag, length), :]
+                    total = total + tap * proj[mb, stream * blocks + block, pl.ds(PAD - lag, length), :]
                 return total
 
             query, key, value = featured(0), featured(1), featured(2)
@@ -235,10 +243,10 @@
                     tap = taps[lag * 3 + stream, :, lanes]
                     total = total + tap * turn[stream * blocks + block, pl.ds(lag, length), :]
                 rows = pl.ds(pl.multiple_of(stream * width + block * 128, 128), 128)
-                grad_t[rows, :] = jnp.transpose(total).astype(BF16)
+                grad_t[mb, rows, :] = jnp.transpose(total).astype(BF16)
             return carry
 
-        lax.fori_loop(begin, end, one_block, 0)
+        lax.fori_loop(2 * half, 2 * half + 2, one_block, 0)
 
     def sum_copy(mb, cls, key, hop):
         return pltpu.make_async_remote_copy(
@@ -256,26 +264,27 @@
         copy.start()
         sent.append(copy)
 
-    def share(mb, *keys):
-        for key in keys:
-            rows = rows_of(device_at(*key), 0, width)
-            total = None
-            for stream in range(3):
-                part = jnp.dot(
-                    w[stream, rows, :], grad_t[stream * width : stream * width + width, :], preferred_element_type=F32
-                )
-                total = part if total is None else total + part
-            for cls in range(2):
-                piece = total[cls * HALF : cls * HALF + HALF, :]
-                hop, joins = returns(mb, cls, key)
-                if hop is not None and not joins:
-                    push_sum(mb, cls, key, hop, piece)
-                else:
-                    partial[cls, slot(key)] = piece
-
-    def combine(mb, cls, key):
+    def share(mb, dx, dy):
+        key = (dx, dy)
+        rows = rows_of(device_at(*key), 0, width)
+        total = None
+        for stream in range(3):
+            part = jnp.dot(
+                w[stream, rows, :], grad_t[mb, stream * width : stream * width + width, :], preferred_element_type=F32
+            )
+            total = part if total is None else total + part
+        for cls in range(2):
+            piece = total[cls * HALF : cls * HALF + HALF, :]
+            hop, joins = returns(mb, cls, key)
+            if hop is not None and not joins:
+                push_sum(mb, cls, key, hop, piece)
+            else:
+                partial[mb, cls, slot(key)] = piece
+
+    def combine(mb, cls, dx, dy):
+        key = (dx, dy)
         hop, joins = returns(mb, cls, key)
-        total = partial[cls, slot(key)]
+        total = partial[mb, cls, slot(key)]
         for join in joins:
             sum_copy(mb, cls, join, RIGHT).wait_recv()
             total = total + recvbuf[mb, cls, slot(join)].astype(F32)
@@ -296,67 +305,106 @@
         ended.append(copy)
 
     ended = []
-    group_a = [(1, (0, 1)), (0, (1, 0)), (0, (3, 0)), (1, (1, 0))]
-    group_b = [(1, (3, 1)), (0, (2, 0))]
-    group_c = [(1, (3, 0)), (0, (0, 1))]
-    group_d = [(1, (1, 1)), (0, (1, 1)), (0, (3, 1)), (1, (2, 0))]
-    group_e = [(1, (2, 1)), (0, (2, 1))]
-    owned = [(0, (0, 0)), (1, (0, 0))]
-
-    gather_start(0)
-    build_tables(0, 12)
-    w_copy((0, 0)).wait()
-    project(0, owned, first=True)
-    gather_handle(0, *group_a)
-    gather_start(1)
-    for key in arrival[1:]:
-        w_copy(key).wait()
-    project(0, group_a)
-    gather_handle(0, *group_b)
-    build_tables(12, 22)
-    gather_handle(0, *group_c)
-    project(0, group_b + group_c)
-    build_tables(22, 32)
-    gather_handle(0, *group_d)
-    project(0, group_d)
-    gather_handle(1, *group_a)
-    gather_handle(0, *group_e)
-    project(0, group_e)
-    for copy in small[1:]:
-        copy.wait()
-    mixer(0, 0, 2)
-    gather_handle(1, *group_b)
-    mixer(0, 2, 4)
-    share(0, (2, 1), (2, 0), (1, 1), (3, 1), (0, 1), (3, 0), (1, 0), (0, 0))
-    project(1, owned, first=True)
-    project(1, group_a)
-    combine(0, 0, (2, 0))
-    combine(0, 1, (1, 0))
-    combine(0, 1, (3, 1))
-    gather_handle(1, *group_c)
-    project(1, group_b + group_c)
-    combine(0, 0, (3, 0))
-    combine(0, 0, (1, 0))
-    combine(0, 1, (0, 1))
-    gather_handle(1, *group_d)
-    project(1, group_d)
-    gather_handle(1, *group_e)
-    project(1, group_e)
-    mixer(1, 0, 2)
-    combine(0, 0, (0, 0))
-    combine(0, 1, (0, 0))
-    mixer(1, 2, 4)
-    share(1, (2, 1), (2, 0), (1, 1), (3, 1))
-    combine(1, 0, (2, 0))
-    combine(1, 1, (3, 1))
-    share(1, (0, 1), (3, 0), (1, 0))
-    combine(1, 1, (1, 0))
-    combine(1, 0, (1, 0))
-    combine(1, 0, (3, 0))
-    combine(1, 1, (0, 1))
-    share(1, (0, 0))
-    combine(1, 0, (0, 0))
-    combine(1, 1, (0, 0))
+    origin(1, 0, 1)
+    origin(1, 1, 0)
+    origin(1, 0, 0)
+    origin(0, 0, 0)
+    origin(1, 1, 2)
+    origin(1, 1, 1)
+    origin(0, 0, 1)
+    build_tables(1)
+    origin(0, 0, 2)
+    build_tables(0)
+    origin(0, 1, 0)
+    build_tables(3)
+    origin(1, 0, 2)
+    handle(1, 0, 3, 0)
+    handle(1, 1, 0, 1)
+    build_tables(2)
+    origin(0, 1, 2)
+    handle(1, 0, 1, 0)
+    build_tables(4)
+    project(1, 0, 0)
+    origin(0, 1, 1)
+    handle(0, 0, 0, 1)
+    project(0, 0, 0)
+    handle(0, 0, 1, 0)
+    handle(1, 1, 1, 0)
+    build_tables(6)
+    handle(0, 1, 0, 1)
+    handle(1, 0, 2, 0)
+    project(0, 0, 1)
+    build_tables(5)
+    handle(0, 0, 3, 0)
+    handle(1, 1, 3, 1)
+    handle(0, 1, 1, 0)
+    handle(1, 0, 3, 1)
+    project(1, 1, 0)
+    handle(1, 1, 3, 0)
+    project(0, 1, 0)
+    handle(0, 1, 3, 0)
+    handle(1, 0, 0, 1)
+    project(1, 3, 1)
+    handle(1, 0, 1, 1)
+    project(0, 3, 0)
+    project(1, 0, 1)
+    build_tables(7)
+    handle(0, 0, 2, 0)
+    handle(0, 1, 3, 1)
+    handle(1, 1, 1, 1)
+    project(1, 3, 0)
+    handle(1, 1, 2, 0)
+    project(1, 1, 1)
+    project(1, 2, 0)
+    handle(1, 0, 2, 1)
+    handle(1, 1, 2, 1)
+    project(1, 2, 1)
+    mixer(1, 1)
+    handle(0, 0, 3, 1)
+    handle(0, 1, 1, 1)
+    mixer(1, 0)
+    handle(0, 0, 1, 1)
+    handle(0, 1, 2, 0)
+    project(0, 1, 1)
+    handle(0, 0, 2, 1)
+    project(0, 3, 1)
+    share(1, 2, 1)
+    project(0, 2, 0)
+    handle(0, 1, 2, 1)
+    share(1, 1, 1)
+    project(0, 2, 1)
+    mixer(0, 0)
+    mixer(0, 1)
+    share(0, 2, 1)
+    share(1, 2, 0)
+    combine(1, 0, 2, 0)
+    share(1, 3, 1)
+    share(0, 1, 1)
+    share(1, 1, 0)
+    share(0, 2, 0)
+    combine(1, 1, 3, 1)
+    share(0, 3, 1)
+    combine(1, 0, 1, 0)
+    share(1, 0, 1)
+    combine(0, 1, 3, 1)
+    share(1, 3, 0)
+    combine(0, 0, 2, 0)
+    share(0, 0, 1)
+    combine(1, 1, 1, 0)
+    combine(1, 0, 3, 0)
+    share(0, 3, 0)
+    combine(1, 1, 0, 1)
+    share(0, 1, 0)
+    share(1, 0, 0)
+    combine(0, 1, 1, 0)
+    combine(0, 1, 0, 1)
+    combine(0, 0, 3, 0)
+    combine(0, 0, 1, 0)
+    share(0, 0, 0)
+    combine(1, 0, 0, 0)
+    combine(1, 1, 0, 0)
+    combine(0, 1, 0, 0)
+    combine(0, 0, 0, 0)
     for copy in sent:
         copy.wait_send()
     for copy in ended:
@@ -387,12 +435,12 @@
             pltpu.VMEM((groups, 128), F32),
             pltpu.VMEM((groups, 128), F32),
             pltpu.VMEM((1, width), F32),
+            pltpu.VMEM((micro, parts, length + PAD, 128), F32),
             pltpu.VMEM((parts, length + PAD, 128), F32),
-            pltpu.VMEM((parts, length + PAD, 128), F32),
-            pltpu.VMEM((3 * width, length), BF16),
+            pltpu.VMEM((micro, 3 * width, length), BF16),
             pltpu.VMEM((groups * 128, 256), BF16),
             pltpu.VMEM((groups * 128, 256), BF16),
-            pltpu.VMEM((2, 8, HALF, length), F32),
+            pltpu.VMEM((micro, 2, 8, HALF, length), F32),
             pltpu.VMEM((micro, 2, 8, HALF, length), BF16),
             pltpu.VMEM((micro, 2, 8, HALF, length), BF16),
             pltpu.VMEM((micro, 2, length, HALF), BF16),

time: 62.9 us -> 53.2 us (0.85)
  Pallas kernels: 60.7 us -> 51.2 us
    pallas_call x1, Pallas kernels: 60.7 us -> 51.2 us  [local(): pl.pallas_call(functools.partial(kernel, sections), out_shape=jax.ShapeDt...]
where the time goes in v3:
time: 53.2 us; the launch traced here: 52.8 us
  Pallas kernels  51.2 us (96%)
  local copies, waits for them, and re-layouts  1.67 us (3%)
    pallas_call x1, Pallas kernels, local(): pl.pallas_call(functools.partial(kernel, sections), out_shape=jax.ShapeDt...  51.2 us
    unnamed x1, local copies, waits for them, and re-layouts  1.67 us

profile of v3, /device:TPU:1, one launch (start us, length us, event | category | flops | bytes accessed | tf_op | source)
XLA Modules:
  0.0 52.8 jit_solution(10824616876911870921)
XLA Ops:
  0.0 51.2 %shard_map.64 = bf16[1,2,128,512]{3,2,1,0:T(8,128)(2,1)} custom-call(bf16[1,2,128,512]{3,2,1,0:T(8,128)(2,1)} %x_hbm.1, bf16[1,2,128,512]{3,2,1,0:T(8,128)(2,1)} %inc_hbm.1, bf16[1,3,4096,512]{3,2,1,0:T(8,128)(2,1)} %bitcast.3, f32[21,1,512]{2,1,0:T(1,128)} %bitcast.4, f32[1,32,128]{2,1,0:T(8,128)} %bitcast.5, f32[1,512]{1,0:T(1,128)} %skip_hbm.1), custom_call_target="tpu_custom_call" | custom-call | tf_op jit(solution)/shard_map/pallas_call | solution.py:425
  51.2 1.7 %copy.8 = bf16[1,2,128,512]{3,2,1,0:T(8,128)(2,1)} copy(bf16[1,2,128,512]{3,2,1,0:T(8,128)(2,1)} %shard_map.64) | data formatting | bytes 524288

commit v4 on v3

--- a/solution.py
+++ b/solution.py
@@ -118,7 +118,7 @@
         for cls in range(2):
             own_x[mb][cls].start()
     small[0].start()
-    arrival = [(0, 0), (0, 1), (1, 0), (3, 0), (1, 1), (3, 1), (2, 0), (2, 1)]
+    arrival = [(0, 0), (3, 1), (1, 0), (3, 0), (0, 1), (1, 1), (2, 0), (2, 1)]
     for key in arrival:
         w_copy(key).start()
     for copy in small[1:]:
@@ -181,8 +181,8 @@
         begun.add(mb)
 
     def build_tables(number):
-        def build(group, carry):
-            rows = pl.ds(pl.multiple_of(group * 128, 128), 128)
+        for group in range(4 * number, 4 * number + 4):
+            rows = pl.ds(group * 128, 128)
             ahead = jnp.broadcast_to(medium[pl.ds(group, 1), :], (128, 128))
             ahead = pltpu.roll(ahead, 0, 1, stride=1, stride_axis=0)
             high, low = split_two(jnp.where(place_c >= place_r, ahead, 0.0))
@@ -193,15 +193,12 @@
             high, low = split_two(jnp.where(place_c <= place_r, behind, 0.0))
             fwd_t[rows, 0:128] = high
             fwd_t[rows, 128:256] = low
-            return carry
-
-        lax.fori_loop(4 * number, 4 * number + 4, build, 0)
 
     def medium_conv(table, block, value):
         high, low = split_two(value)
         both = jnp.concatenate([high, low], axis=1)
         both = jnp.concatenate([both, both], axis=0)
-        rows = pl.ds(pl.multiple_of(block * 1024, 1024), 1024)
+        rows = pl.ds(block * 1024, 1024)
         raw = jnp.dot(table[rows, :], both, preferred_element_type=F32)
         lane_group = lax.div(place_c, 16)
         total = raw[0:length, 0:128] + raw[0:length, 128:256]
@@ -217,8 +214,8 @@
         while len(ready) < len(small) - 1:
             ready.append(small[len(ready) + 1].wait())
 
-        def one_block(block, carry):
-            lanes = pl.ds(pl.multiple_of(block * 128, 128), 128)
+        def one_block(block):
+            lanes = pl.ds(block * 128, 128)
 
             def featured(stream):
                 total = jnp.zeros((length, 128), F32)
@@ -242,11 +239,11 @@
                 for lag in range(7):
                     tap = taps[lag * 3 + stream, :, lanes]
                     total = total + tap * turn[stream * blocks + block, pl.ds(lag, length), :]
-                rows = pl.ds(pl.multiple_of(stream * width + block * 128, 128), 128)
+                rows = pl.ds(stream * width + block * 128, 128)
                 grad_t[mb, rows, :] = jnp.transpose(total).astype(BF16)
-            return carry
-
-        lax.fori_loop(2 * half, 2 * half + 2, one_block, 0)
+
+        for block in range(2 * half, 2 * half + 2):
+            one_block(block)
 
     def sum_copy(mb, cls, key, hop):
         return pltpu.make_async_remote_copy(
@@ -305,106 +302,106 @@
         ended.append(copy)
 
     ended = []
+    origin(0, 0, 1)
+    origin(0, 1, 0)
     origin(1, 0, 1)
+    origin(0, 0, 0)
+    origin(0, 1, 1)
+    origin(1, 1, 2)
+    project(0, 0, 0)
+    origin(0, 1, 2)
+    origin(1, 1, 1)
+    origin(0, 0, 2)
     origin(1, 1, 0)
+    build_tables(5)
+    build_tables(2)
+    project(1, 0, 0)
+    build_tables(6)
+    build_tables(4)
+    build_tables(0)
+    handle(0, 0, 3, 0)
+    handle(0, 0, 1, 0)
+    handle(0, 1, 0, 1)
+    build_tables(7)
+    origin(1, 0, 2)
     origin(1, 0, 0)
-    origin(0, 0, 0)
-    origin(1, 1, 2)
-    origin(1, 1, 1)
-    origin(0, 0, 1)
+    handle(0, 0, 0, 1)
+    handle(0, 1, 1, 0)
+    handle(1, 0, 3, 0)
     build_tables(1)
-    origin(0, 0, 2)
-    build_tables(0)
-    origin(0, 1, 0)
-    build_tables(3)
-    origin(1, 0, 2)
-    handle(1, 0, 3, 0)
     handle(1, 1, 0, 1)
-    build_tables(2)
-    origin(0, 1, 2)
-    handle(1, 0, 1, 0)
-    build_tables(4)
-    project(1, 0, 0)
-    origin(0, 1, 1)
-    handle(0, 0, 0, 1)
-    project(0, 0, 0)
-    handle(0, 0, 1, 0)
-    handle(1, 1, 1, 0)
-    build_tables(6)
-    handle(0, 1, 0, 1)
-    handle(1, 0, 2, 0)
-    project(0, 0, 1)
-    build_tables(5)
-    handle(0, 0, 3, 0)
-    handle(1, 1, 3, 1)
-    handle(0, 1, 1, 0)
-    handle(1, 0, 3, 1)
-    project(1, 1, 0)
+    handle(0, 0, 3, 1)
     handle(1, 1, 3, 0)
-    project(0, 1, 0)
-    handle(0, 1, 3, 0)
-    handle(1, 0, 0, 1)
-    project(1, 3, 1)
-    handle(1, 0, 1, 1)
-    project(0, 3, 0)
-    project(1, 0, 1)
-    build_tables(7)
+    project(1, 3, 0)
     handle(0, 0, 2, 0)
     handle(0, 1, 3, 1)
-    handle(1, 1, 1, 1)
-    project(1, 3, 0)
-    handle(1, 1, 2, 0)
-    project(1, 1, 1)
-    project(1, 2, 0)
-    handle(1, 0, 2, 1)
-    handle(1, 1, 2, 1)
-    project(1, 2, 1)
-    mixer(1, 1)
-    handle(0, 0, 3, 1)
+    project(0, 3, 1)
+    handle(0, 0, 1, 1)
+    handle(1, 1, 1, 0)
+    build_tables(3)
+    handle(0, 1, 3, 0)
+    project(0, 1, 0)
+    project(0, 3, 0)
+    handle(1, 0, 0, 1)
+    handle(1, 0, 2, 0)
+    project(1, 0, 1)
     handle(0, 1, 1, 1)
-    mixer(1, 0)
-    handle(0, 0, 1, 1)
+    project(0, 0, 1)
+    project(0, 1, 1)
+    handle(1, 1, 3, 1)
+    handle(1, 0, 1, 0)
     handle(0, 1, 2, 0)
-    project(0, 1, 1)
-    handle(0, 0, 2, 1)
-    project(0, 3, 1)
-    share(1, 2, 1)
+    handle(1, 0, 3, 1)
+    project(1, 3, 1)
+    project(1, 1, 0)
     project(0, 2, 0)
     handle(0, 1, 2, 1)
+    handle(0, 0, 2, 1)
+    project(0, 2, 1)
+    mixer(0, 1)
+    mixer(0, 0)
+    share(0, 1, 1)
+    share(0, 2, 1)
+    handle(1, 1, 2, 1)
+    handle(1, 1, 2, 0)
+    handle(1, 0, 2, 1)
+    project(1, 2, 0)
+    handle(1, 0, 1, 1)
+    handle(1, 1, 1, 1)
+    project(1, 2, 1)
+    project(1, 1, 1)
+    mixer(1, 0)
+    mixer(1, 1)
+    share(1, 2, 1)
+    share(0, 2, 0)
+    share(1, 3, 1)
+    share(0, 3, 1)
+    combine(0, 1, 3, 1)
+    combine(0, 0, 2, 0)
+    share(1, 3, 0)
+    share(1, 2, 0)
+    share(0, 1, 0)
     share(1, 1, 1)
-    project(0, 2, 1)
-    mixer(0, 0)
-    mixer(0, 1)
-    share(0, 2, 1)
-    share(1, 2, 0)
+    combine(1, 1, 3, 1)
+    share(0, 0, 1)
     combine(1, 0, 2, 0)
-    share(1, 3, 1)
-    share(0, 1, 1)
-    share(1, 1, 0)
-    share(0, 2, 0)
-    combine(1, 1, 3, 1)
-    share(0, 3, 1)
-    combine(1, 0, 1, 0)
-    share(1, 0, 1)
-    combine(0, 1, 3, 1)
-    share(1, 3, 0)
-    combine(0, 0, 2, 0)
-    share(0, 0, 1)
-    combine(1, 1, 1, 0)
-    combine(1, 0, 3, 0)
-    share(0, 3, 0)
-    combine(1, 1, 0, 1)
-    share(0, 1, 0)
-    share(1, 0, 0)
     combine(0, 1, 1, 0)
     combine(0, 1, 0, 1)
+    share(1, 0, 1)
+    share(0, 3, 0)
+    share(1, 1, 0)
+    combine(0, 0, 1, 0)
     combine(0, 0, 3, 0)
-    combine(0, 0, 1, 0)
     share(0, 0, 0)
-    combine(1, 0, 0, 0)
-    combine(1, 1, 0, 0)
+    share(1, 0, 0)
+    combine(1, 1, 1, 0)
+    combine(1, 1, 0, 1)
+    combine(1, 0, 1, 0)
+    combine(1, 0, 3, 0)
     combine(0, 1, 0, 0)
     combine(0, 0, 0, 0)
+    combine(1, 1, 0, 0)
+    combine(1, 0, 0, 0)
     for copy in sent:
         copy.wait_send()
     for copy in ended:

time: 53.2 us -> 51.2 us (0.962)
  Pallas kernels: 51.2 us -> 48.8 us
    pallas_call x1, Pallas kernels: 51.2 us -> 48.8 us  [local(): pl.pallas_call(functools.partial(kernel, sections), out_shape=jax.ShapeDt...]
where the time goes in v4:
time: 51.2 us; the launch traced here: 50.5 us
  Pallas kernels  48.8 us (95%)
  local copies, waits for them, and re-layouts  1.67 us (3%)
    pallas_call x1, Pallas kernels, local(): pl.pallas_call(functools.partial(kernel, sections), out_shape=jax.ShapeDt...  48.8 us
    unnamed x1, local copies, waits for them, and re-layouts  1.67 us

profile of v4, /device:TPU:1, one launch (start us, length us, event | category | flops | bytes accessed | tf_op | source)
XLA Modules:
  0.0 50.5 jit_solution(10317920800938289872)
XLA Ops:
  0.0 48.8 %shard_map.64 = bf16[1,2,128,512]{3,2,1,0:T(8,128)(2,1)} custom-call(bf16[1,2,128,512]{3,2,1,0:T(8,128)(2,1)} %x_hbm.1, bf16[1,2,128,512]{3,2,1,0:T(8,128)(2,1)} %inc_hbm.1, bf16[1,3,4096,512]{3,2,1,0:T(8,128)(2,1)} %bitcast.3, f32[21,1,512]{2,1,0:T(1,128)} %bitcast.4, f32[1,32,128]{2,1,0:T(8,128)} %bitcast.5, f32[1,512]{1,0:T(1,128)} %skip_hbm.1), custom_call_target="tpu_custom_call" | custom-call | tf_op jit(solution)/shard_map/pallas_call | solution.py:422
  48.9 1.7 %copy.8 = bf16[1,2,128,512]{3,2,1,0:T(8,128)(2,1)} copy(bf16[1,2,128,512]{3,2,1,0:T(8,128)(2,1)} %shard_map.64) | data formatting | bytes 524288

commit v5 on v4

--- a/solution.py
+++ b/solution.py
@@ -417,6 +417,10 @@
     taps = jnp.transpose(short_taps, (1, 2, 0, 3)).reshape(lags * 3, 1, width)
     medium = jnp.transpose(medium_taps, (0, 2, 1))
     parts = 3 * (width // 128)
+    block_input, incoming, taps, medium, skip_weight = (
+        pltpu.with_memory_space_constraint(value, pltpu.HBM)
+        for value in (block_input, incoming, taps, medium, skip_weight)
+    )
     anywhere = pl.BlockSpec(memory_space=pl.ANY)
     dma = pltpu.SemaphoreType.DMA
     return pl.pallas_call(
@@ -451,7 +455,7 @@
             dma((micro, 2)),
         ],
         compiler_params=pltpu.CompilerParams(
-            collective_id=0, has_side_effects=True, vmem_limit_bytes=56 * 1024 * 1024
+            collective_id=0, has_side_effects=True, vmem_limit_bytes=48 * 1024 * 1024
         ),
     )(block_input, incoming, weights, taps, medium, skip_weight)
 

time: 51.2 us -> 50.1 us (0.979)
  local copies, waits for them, and re-layouts: 1.67 us -> 0.71 us
    unnamed x1, local copies, waits for them, and re-layouts: 1.67 us -> 0.71 us
where the time goes in v5:
time: 50.1 us; the launch traced here: 49.5 us
  Pallas kernels  48.7 us (97%)
  local copies, waits for them, and re-layouts  0.71 us (1%)
    pallas_call x1, Pallas kernels, local(): pl.pallas_call(functools.partial(kernel, sections), out_shape=jax.ShapeDt...  48.7 us

profile of v5, /device:TPU:1, one launch (start us, length us, event | category | flops | bytes accessed | tf_op | source)
XLA Modules:
  0.0 49.5 jit_solution(2633638628189368344)
XLA Ops:
  0.0 48.7 %shard_map.64 = bf16[1,2,128,512]{3,2,1,0:T(8,128)(2,1)S(1)} custom-call(bf16[1,2,128,512]{3,2,1,0:T(8,128)(2,1)} %x_hbm.1, bf16[1,2,128,512]{3,2,1,0:T(8,128)(2,1)} %inc_hbm.1, bf16[1,3,4096,512]{3,2,1,0:T(8,128)(2,1)} %bitcast.3, f32[21,1,512]{2,1,0:T(1,128)} %bitcast.4, f32[1,32,128]{2,1,0:T(8,128)} %bitcast.5, f32[1,512]{1,0:T(1,128)} %skip_hbm.1), custom_call_target="tpu_custom_call" | custom-call | tf_op jit(solution)/shard_map/pallas_call | solution.py:426
  48.8 0.7 %copy.8 = bf16[1,2,128,512]{3,2,1,0:T(8,128)(2,1)} copy(bf16[1,2,128,512]{3,2,1,0:T(8,128)(2,1)S(1)} %shard_map.64) | data formatting | bytes 524288

commit v6 on v5

--- a/solution.py
+++ b/solution.py
@@ -29,6 +29,9 @@
             (2, 0): [(ACROSS, (2, 1))],
         }
         table[far].insert(0, (far, (2, 0)))
+        if mb == 0:
+            del table[(2, 0)]
+            table[(3, 1)] = [(LEFT, (2, 1))]
     else:
         table = {
             (0, 1): [(RIGHT, (1, 1)), (LEFT, (3, 1))],
@@ -41,10 +44,12 @@
 def returns(mb, cls, key):
     if cls == 0:
         far = RIGHT if mb == 0 else LEFT
+        if mb == 0 and key == (2, 1):
+            return RIGHT, []
         if key[1] == 1:
-            return ACROSS, []
+            return ACROSS, [(2, 1)] if mb == 0 and key == (1, 1) else []
         if key == (2, 0):
-            return far, [(2, 1)]
+            return far, [] if mb == 0 else [(2, 1)]
         if key == (0, 0):
             return None, [(0, 1), (1, 0), (3, 0)]
         return key, [(key[0], 1)] + ([(2, 0)] if key == far else [])
@@ -118,7 +123,7 @@
         for cls in range(2):
             own_x[mb][cls].start()
     small[0].start()
-    arrival = [(0, 0), (3, 1), (1, 0), (3, 0), (0, 1), (1, 1), (2, 0), (2, 1)]
+    arrival = [(0, 0), (0, 1), (1, 0), (3, 0), (3, 1), (1, 1), (2, 0), (2, 1)]
     for key in arrival:
         w_copy(key).start()
     for copy in small[1:]:
@@ -302,106 +307,106 @@
         ended.append(copy)
 
     ended = []
+    origin(1, 0, 1)
+    origin(1, 1, 0)
     origin(0, 0, 1)
+    origin(1, 1, 1)
+    build_tables(7)
+    origin(0, 1, 2)
     origin(0, 1, 0)
-    origin(1, 0, 1)
+    build_tables(5)
+    origin(1, 0, 0)
+    origin(0, 0, 2)
+    build_tables(4)
+    origin(1, 0, 2)
     origin(0, 0, 0)
     origin(0, 1, 1)
+    build_tables(2)
+    handle(1, 0, 3, 0)
+    handle(1, 1, 0, 1)
+    handle(1, 1, 1, 0)
+    handle(0, 1, 0, 1)
+    project(1, 0, 0)
     origin(1, 1, 2)
+    handle(0, 0, 3, 0)
+    build_tables(3)
     project(0, 0, 0)
-    origin(0, 1, 2)
-    origin(1, 1, 1)
-    origin(0, 0, 2)
-    origin(1, 1, 0)
-    build_tables(5)
-    build_tables(2)
-    project(1, 0, 0)
-    build_tables(6)
-    build_tables(4)
+    handle(1, 0, 1, 0)
     build_tables(0)
-    handle(0, 0, 3, 0)
-    handle(0, 0, 1, 0)
-    handle(0, 1, 0, 1)
-    build_tables(7)
-    origin(1, 0, 2)
-    origin(1, 0, 0)
+    handle(1, 0, 2, 0)
+    handle(1, 0, 0, 1)
     handle(0, 0, 0, 1)
     handle(0, 1, 1, 0)
-    handle(1, 0, 3, 0)
+    project(1, 0, 1)
+    handle(0, 1, 3, 0)
+    project(0, 0, 1)
+    handle(1, 1, 3, 1)
+    handle(1, 0, 3, 1)
+    handle(0, 0, 1, 0)
+    project(1, 3, 1)
+    project(1, 1, 0)
+    project(0, 1, 0)
+    handle(0, 0, 3, 1)
+    project(0, 3, 0)
+    build_tables(6)
+    handle(0, 1, 3, 1)
+    project(0, 3, 1)
     build_tables(1)
-    handle(1, 1, 0, 1)
-    handle(0, 0, 3, 1)
+    handle(1, 1, 1, 1)
+    handle(1, 0, 1, 1)
+    handle(1, 1, 2, 0)
+    project(1, 1, 1)
+    project(1, 2, 0)
     handle(1, 1, 3, 0)
     project(1, 3, 0)
-    handle(0, 0, 2, 0)
-    handle(0, 1, 3, 1)
-    project(0, 3, 1)
-    handle(0, 0, 1, 1)
-    handle(1, 1, 1, 0)
-    build_tables(3)
-    handle(0, 1, 3, 0)
-    project(0, 1, 0)
-    project(0, 3, 0)
-    handle(1, 0, 0, 1)
-    handle(1, 0, 2, 0)
-    project(1, 0, 1)
-    handle(0, 1, 1, 1)
-    project(0, 0, 1)
-    project(0, 1, 1)
-    handle(1, 1, 3, 1)
-    handle(1, 0, 1, 0)
-    handle(0, 1, 2, 0)
-    handle(1, 0, 3, 1)
-    project(1, 3, 1)
-    project(1, 1, 0)
-    project(0, 2, 0)
-    handle(0, 1, 2, 1)
-    handle(0, 0, 2, 1)
-    project(0, 2, 1)
-    mixer(0, 1)
-    mixer(0, 0)
-    share(0, 1, 1)
-    share(0, 2, 1)
     handle(1, 1, 2, 1)
-    handle(1, 1, 2, 0)
     handle(1, 0, 2, 1)
-    project(1, 2, 0)
-    handle(1, 0, 1, 1)
-    handle(1, 1, 1, 1)
     project(1, 2, 1)
-    project(1, 1, 1)
     mixer(1, 0)
     mixer(1, 1)
+    share(1, 2, 0)
     share(1, 2, 1)
+    handle(0, 1, 2, 0)
+    share(1, 1, 1)
+    handle(0, 0, 1, 1)
+    handle(0, 0, 2, 1)
+    handle(0, 0, 2, 0)
+    handle(0, 1, 1, 1)
+    handle(0, 1, 2, 1)
+    project(0, 1, 1)
+    project(0, 2, 0)
+    project(0, 2, 1)
+    mixer(0, 0)
+    mixer(0, 1)
+    share(0, 2, 1)
+    share(1, 3, 1)
     share(0, 2, 0)
-    share(1, 3, 1)
+    combine(1, 1, 3, 1)
     share(0, 3, 1)
+    combine(1, 0, 2, 0)
+    share(0, 1, 0)
+    share(1, 0, 1)
+    share(1, 1, 0)
+    share(0, 1, 1)
     combine(0, 1, 3, 1)
-    combine(0, 0, 2, 0)
+    combine(0, 0, 1, 1)
+    combine(1, 1, 1, 0)
     share(1, 3, 0)
-    share(1, 2, 0)
-    share(0, 1, 0)
-    share(1, 1, 1)
-    combine(1, 1, 3, 1)
+    combine(1, 1, 0, 1)
     share(0, 0, 1)
-    combine(1, 0, 2, 0)
-    combine(0, 1, 1, 0)
-    combine(0, 1, 0, 1)
-    share(1, 0, 1)
-    share(0, 3, 0)
-    share(1, 1, 0)
-    combine(0, 0, 1, 0)
-    combine(0, 0, 3, 0)
-    share(0, 0, 0)
-    share(1, 0, 0)
-    combine(1, 1, 1, 0)
-    combine(1, 1, 0, 1)
     combine(1, 0, 1, 0)
     combine(1, 0, 3, 0)
+    combine(0, 1, 1, 0)
+    share(0, 3, 0)
+    share(1, 0, 0)
+    combine(0, 1, 0, 1)
+    combine(0, 0, 3, 0)
+    combine(0, 0, 1, 0)
+    share(0, 0, 0)
+    combine(1, 1, 0, 0)
+    combine(1, 0, 0, 0)
     combine(0, 1, 0, 0)
     combine(0, 0, 0, 0)
-    combine(1, 1, 0, 0)
-    combine(1, 0, 0, 0)
     for copy in sent:
         copy.wait_send()
     for copy in ended:

time: 50.1 us -> 49.4 us (0.986)
  Pallas kernels: 48.7 us -> 48.1 us
    pallas_call x1, Pallas kernels: 48.7 us -> 48.1 us  [local(): pl.pallas_call(functools.partial(kernel, sections), out_shape=jax.ShapeDt...]
where the time goes in v6:
time: 49.4 us; the launch traced here: 48.9 us
  Pallas kernels  48.1 us (97%)
  local copies, waits for them, and re-layouts  0.71 us (1%)
    pallas_call x1, Pallas kernels, local(): pl.pallas_call(functools.partial(kernel, sections), out_shape=jax.ShapeDt...  48.1 us

profile of v6, /device:TPU:1, one launch (start us, length us, event | category | flops | bytes accessed | tf_op | source)
XLA Modules:
  0.0 48.9 jit_solution(14100802605340797090)
XLA Ops:
  0.0 48.1 %shard_map.64 = bf16[1,2,128,512]{3,2,1,0:T(8,128)(2,1)S(1)} custom-call(bf16[1,2,128,512]{3,2,1,0:T(8,128)(2,1)} %x_hbm.1, bf16[1,2,128,512]{3,2,1,0:T(8,128)(2,1)} %inc_hbm.1, bf16[1,3,4096,512]{3,2,1,0:T(8,128)(2,1)} %bitcast.3, f32[21,1,512]{2,1,0:T(1,128)} %bitcast.4, f32[1,32,128]{2,1,0:T(8,128)} %bitcast.5, f32[1,512]{1,0:T(1,128)} %skip_hbm.1), custom_call_target="tpu_custom_call" | custom-call | tf_op jit(solution)/shard_map/pallas_call | solution.py:431
  48.2 0.7 %copy.8 = bf16[1,2,128,512]{3,2,1,0:T(8,128)(2,1)} copy(bf16[1,2,128,512]{3,2,1,0:T(8,128)(2,1)S(1)} %shard_map.64) | data formatting | bytes 524288

commit v7 on v6

--- a/solution.py
+++ b/solution.py
@@ -131,13 +131,6 @@
 
     place_r = lax.broadcasted_iota(jnp.int32, (128, 128), 0)
     place_c = lax.broadcasted_iota(jnp.int32, (128, 128), 1)
-    small[0].wait()
-    flip = jnp.where(lax.rem(place_r + place_c, 128) == 0, 1.0, 0.0).astype(F32)
-    flipped[...] = jnp.dot(medium[...], flip, precision=lax.Precision.HIGHEST, preferred_element_type=F32)
-    for part in range(3 * blocks):
-        for mb in range(micro):
-            proj[mb, part, 0:PAD, :] = jnp.zeros((PAD, 128), F32)
-        turn[part, length : length + PAD, :] = jnp.zeros((PAD, 128), F32)
     for mb in range(micro):
         for cls in range(2):
             own_x[mb][cls].wait()
@@ -185,7 +178,21 @@
                 proj[where] = proj[where] + piece if mb in begun else piece
         begun.add(mb)
 
+    begun_tables = []
+
+    def prepare():
+        small[0].wait()
+        flip = jnp.where(lax.rem(place_r + place_c, 128) == 0, 1.0, 0.0).astype(F32)
+        flipped[...] = jnp.dot(medium[...], flip, precision=lax.Precision.HIGHEST, preferred_element_type=F32)
+        for part in range(3 * blocks):
+            for mb in range(micro):
+                proj[mb, part, 0:PAD, :] = jnp.zeros((PAD, 128), F32)
+            turn[part, length : length + PAD, :] = jnp.zeros((PAD, 128), F32)
+
     def build_tables(number):
+        if not begun_tables:
+            prepare()
+            begun_tables.append(number)
         for group in range(4 * number, 4 * number + 4):
             rows = pl.ds(group * 128, 128)
             ahead = jnp.broadcast_to(medium[pl.ds(group, 1), :], (128, 128))

time: 49.4 us -> 48.8 us (0.988)
  no operation moved by 1% of the time
where the time goes in v7:
time: 48.8 us; the launch traced here: 48.7 us
  Pallas kernels  48 us (98%)
  local copies, waits for them, and re-layouts  0.71 us (1%)
    pallas_call x1, Pallas kernels, local(): pl.pallas_call(functools.partial(kernel, sections), out_shape=jax.ShapeDt...  48 us

profile of v7, /device:TPU:1, one launch (start us, length us, event | category | flops | bytes accessed | tf_op | source)
XLA Modules:
  0.0 48.7 jit_solution(13405621166959513358)
XLA Ops:
  0.0 48.0 %shard_map.64 = bf16[1,2,128,512]{3,2,1,0:T(8,128)(2,1)S(1)} custom-call(bf16[1,2,128,512]{3,2,1,0:T(8,128)(2,1)} %x_hbm.1, bf16[1,2,128,512]{3,2,1,0:T(8,128)(2,1)} %inc_hbm.1, bf16[1,3,4096,512]{3,2,1,0:T(8,128)(2,1)} %bitcast.3, f32[21,1,512]{2,1,0:T(1,128)} %bitcast.4, f32[1,32,128]{2,1,0:T(8,128)} %bitcast.5, f32[1,512]{1,0:T(1,128)} %skip_hbm.1), custom_call_target="tpu_custom_call" | custom-call | tf_op jit(solution)/shard_map/pallas_call | solution.py:438
  48.0 0.7 %copy.8 = bf16[1,2,128,512]{3,2,1,0:T(8,128)(2,1)} copy(bf16[1,2,128,512]{3,2,1,0:T(8,128)(2,1)S(1)} %shard_map.64) | data formatting | bytes 524288

commit v8 on v7

--- a/solution.py
+++ b/solution.py
@@ -318,11 +318,11 @@
     origin(1, 1, 0)
     origin(0, 0, 1)
     origin(1, 1, 1)
-    build_tables(7)
     origin(0, 1, 2)
     origin(0, 1, 0)
     build_tables(5)
     origin(1, 0, 0)
+    build_tables(7)
     origin(0, 0, 2)
     build_tables(4)
     origin(1, 0, 2)

time: 48.8 us -> 48.8 us (level)
  no operation moved by 1% of the time
where the time goes in v8:
time: 48.8 us; the launch traced here: 48.7 us
  Pallas kernels  48 us (98%)
  local copies, waits for them, and re-layouts  0.71 us (1%)
    pallas_call x1, Pallas kernels, local(): pl.pallas_call(functools.partial(kernel, sections), out_shape=jax.ShapeDt...  48 us

profile of v8, /device:TPU:1, one launch (start us, length us, event | category | flops | bytes accessed | tf_op | source)
XLA Modules:
  0.0 48.7 jit_solution(7881104036788211859)
XLA Ops:
  0.0 48.0 %shard_map.64 = bf16[1,2,128,512]{3,2,1,0:T(8,128)(2,1)S(1)} custom-call(bf16[1,2,128,512]{3,2,1,0:T(8,128)(2,1)} %x_hbm.1, bf16[1,2,128,512]{3,2,1,0:T(8,128)(2,1)} %inc_hbm.1, bf16[1,3,4096,512]{3,2,1,0:T(8,128)(2,1)} %bitcast.3, f32[21,1,512]{2,1,0:T(1,128)} %bitcast.4, f32[1,32,128]{2,1,0:T(8,128)} %bitcast.5, f32[1,512]{1,0:T(1,128)} %skip_hbm.1), custom_call_target="tpu_custom_call" | custom-call | tf_op jit(solution)/shard_map/pallas_call | solution.py:438
  48.0 0.7 %copy.8 = bf16[1,2,128,512]{3,2,1,0:T(8,128)(2,1)} copy(bf16[1,2,128,512]{3,2,1,0:T(8,128)(2,1)S(1)} %shard_map.64) | data formatting | bytes 524288
